TPU v7x, 32 devices: a whole 2x2x4 slice. The times are simulated.
32 devices in a mesh: dp: 8 (over y, x, core), tensor: 4 (over z).
Axes of the slice: x: 2, y: 2, z: 4, core: 2. Of those that a mesh axis runs over, the one named last changes fastest.
Arguments:
- hidden_in: bfloat16 [2, 8, 1024, 2048], P(None, None, ('dp', 'tensor')), may hold values from -6 to 6
- lengths: int32 [2, 8], replicated, may hold values from 1 to 1024, 6144 in all within a row
- dealing: int32 [2, 8], replicated, may hold values from 0 to 7, each once within a row
- cotangent: bfloat16 [2, 8, 1024, 2048], P(None, None, ('dp', 'tensor')), may hold values from -6 to 6
- attn_gain: bfloat16 [2048], P(('dp', 'tensor')), may hold values from 0.5 to 1.5
- attn_shift: bfloat16 [2048], P(('dp', 'tensor')), may hold values from -1.5 to 1.5
- ffn_gain: bfloat16 [2048], P(('dp', 'tensor')), may hold values from 0.5 to 1.5
- ffn_shift: bfloat16 [2048], P(('dp', 'tensor')), may hold values from -1.5 to 1.5
- qkv_weight: bfloat16 [2048, 8, 768], P('dp', 'tensor'), may hold values from -0.125 to 0.125
- qkv_bias: bfloat16 [8, 768], P('tensor', 'dp'), may hold values from -0.25 to 0.25
- dense_weight: bfloat16 [8, 256, 2048], P('tensor', 'dp'), may hold values from -1.5 to 1.5
- dense_bias: bfloat16 [2048], P(('dp', 'tensor')), may hold values from -1.5 to 1.5
- fc1_weight: bfloat16 [2048, 8192], P('dp', 'tensor'), may hold values from -0.125 to 0.125
- fc1_bias: bfloat16 [8, 1024], P('tensor', 'dp'), may hold values from -1.5 to 1.5
- fc2_weight: bfloat16 [8192, 2048], P('tensor', 'dp'), may hold values from -0.0625 to 0.0625
- fc2_bias: bfloat16 [2048], P(('dp', 'tensor')), may hold values from -1.5 to 1.5
Outputs:
- output: bfloat16 [2, 8, 1024, 2048], P(None, None, ('dp', 'tensor'))
- input_grad: bfloat16 [2, 8, 1024, 2048], P(None, None, ('dp', 'tensor'))
- attngain_grad: float32 [2048], P(('dp', 'tensor'))
- attnshift_grad: float32 [2048], P(('dp', 'tensor'))
- ffngain_grad: float32 [2048], P(('dp', 'tensor'))
- ffnshift_grad: float32 [2048], P(('dp', 'tensor'))
- qkvweight_grad: float32 [2048, 8, 768], P('dp', 'tensor')
- qkvbias_grad: float32 [8, 768], P('tensor', 'dp')
- denseweight_grad: float32 [8, 256, 2048], P('tensor', 'dp')
- densebias_grad: float32 [2048], P(('dp', 'tensor'))
- fc1weight_grad: float32 [2048, 8192], P('dp', 'tensor')
- fc1bias_grad: float32 [8, 1024], P('tensor', 'dp')
- fc2weight_grad: float32 [8192, 2048], P('tensor', 'dp')
- fc2bias_grad: float32 [2048], P(('dp', 'tensor'))
Inputs may be any that keep to these rules, and one draw needn't show every extreme that they name: lengths[m, j] belongs to the sequence in input slot dealing[m, j]; in each micro-batch the lengths sum to 6144 and the longest is 1024. Each row of dealing holds every slot number once.
All inputs are finite; a program needn't handle non-finite values.
Results may differ from a plain program's by a relative error of at most 0.013.
Values may be sent and summed in bfloat16 or wider, within the bound.
No kernel may reach another device: no remote copies, remote signals or barrier semaphores. Data moves between devices by JAX's collectives and lax.ppermute only.
A program may use at most 320 MiB of HBM per device.

v0:
```python
import math
import jax
import jax.numpy as jnp
from jax import lax
from jax.sharding import PartitionSpec as P

HD = 256
ROT = 64
EPSILON = 1e-05
ROPE_BASE = 10000.0
NEG_FILL = -1e30
SQRT_HALF = 0.7071067811865476
INV_ROOT_TWO_PI = 0.3989422804014327


def normalize(residual, gain, shift):
    centred = residual - jnp.mean(residual, axis=-1, keepdims=True)
    scaling = lax.rsqrt(jnp.mean(centred * centred, axis=-1, keepdims=True) + EPSILON)
    unit_rows = centred * scaling
    return (unit_rows * gain + shift, unit_rows, scaling)


def norm_back(grad_out, unit_rows, scaling, gain):
    grad_unit = grad_out * gain
    return scaling * (
        grad_unit
        - jnp.mean(grad_unit, axis=-1, keepdims=True)
        - unit_rows * jnp.mean(grad_unit * unit_rows, axis=-1, keepdims=True)
    )


def angles(positions):
    freqs = jnp.exp(jnp.arange(ROT // 2, dtype=jnp.float32) * (-2.0 * math.log(ROPE_BASE) / ROT))
    phases = positions.astype(jnp.float32)[:, None] * freqs[None, :]
    return (jnp.cos(phases), jnp.sin(phases))


def rotate(heads, cosines, sines):
    half_rot = ROT // 2
    lead_part = heads[..., :half_rot]
    trail_part = heads[..., half_rot:ROT]
    cos_rows = cosines[:, None, :]
    sin_rows = sines[:, None, :]
    return jnp.concatenate(
        [
            lead_part * cos_rows - trail_part * sin_rows,
            trail_part * cos_rows + lead_part * sin_rows,
            heads[..., ROT:],
        ],
        axis=-1,
    )


def take_slots(table, order):
    return jnp.take(table, order, axis=0)


def per_device(
    hidden_in,
    lengths,
    dealing,
    cotangent,
    attn_gain,
    attn_shift,
    ffn_gain,
    ffn_shift,
    qkv_weight,
    qkv_bias,
    dense_weight,
    dense_bias,
    fc1_weight,
    fc1_bias,
    fc2_weight,
    fc2_bias,
):
    n_tensor = lax.axis_size("tensor")
    n_data = lax.axis_size("dp")
    group_index = lax.axis_index("dp")
    micro_count, seq_count, piece_rows, width = hidden_in.shape
    local_rows = n_data * piece_rows
    seq_rows = n_tensor * local_rows
    block_rows = min(512, seq_rows)
    block_count = seq_rows // block_rows
    scale = 1.0 / math.sqrt(HD)
    sent_in = jax.vmap(take_slots)(hidden_in, dealing)
    sent_grad = jax.vmap(take_slots)(cotangent, dealing)
    got_in, got_grad = (
        lax.all_to_all(sent_in, "dp", split_axis=1, concat_axis=2, tiled=True),
        lax.all_to_all(sent_grad, "dp", split_axis=1, concat_axis=2, tiled=True),
    )
    small = (
        lax.all_gather(attn_gain, ("dp", "tensor"), axis=0, tiled=True),
        lax.all_gather(attn_shift, ("dp", "tensor"), axis=0, tiled=True),
        lax.all_gather(ffn_gain, ("dp", "tensor"), axis=0, tiled=True),
        lax.all_gather(ffn_shift, ("dp", "tensor"), axis=0, tiled=True),
        lax.all_gather(dense_bias, ("dp", "tensor"), axis=0, tiled=True),
        lax.all_gather(fc2_bias, ("dp", "tensor"), axis=0, tiled=True),
    )
    gain_one, shift_one, gain_two, shift_two, dense_shift, fc2_shift = [
        piece.astype(jnp.float32) for piece in small
    ]
    shard_set = (qkv_weight, qkv_bias, dense_weight, fc1_weight, fc1_bias, fc2_weight)

    def current_set():
        return (
            lax.all_gather(shard_set[0], "dp", axis=0, tiled=True),
            lax.all_gather(shard_set[1], "dp", axis=1, tiled=True),
            lax.all_gather(shard_set[2], "dp", axis=1, tiled=True),
            lax.all_gather(shard_set[3], "dp", axis=0, tiled=True),
            lax.all_gather(shard_set[4], "dp", axis=1, tiled=True),
            lax.all_gather(shard_set[5], "dp", axis=1, tiled=True),
        )

    row_ids = jnp.arange(seq_rows, dtype=jnp.int32)
    part_ids = row_ids // local_rows
    within = row_ids % local_rows
    positions = (within // piece_rows * n_tensor + part_ids) * piece_rows + within % piece_rows
    cosines, sines = angles(positions)
    my_lengths = lax.dynamic_index_in_dim(lengths, group_index, axis=1, keepdims=False)
    starts = jnp.arange(block_count, dtype=jnp.int32) * block_rows
    heads_here = qkv_weight.shape[1]
    units_here = fc1_weight.shape[1]
    weight_zero = (
        jnp.zeros((width, heads_here, 3 * HD), jnp.float32),
        jnp.zeros((heads_here, 3 * HD), jnp.float32),
        jnp.zeros((heads_here, HD, width), jnp.float32),
        jnp.zeros((width, units_here), jnp.float32),
        jnp.zeros((heads_here, units_here // heads_here), jnp.float32),
        jnp.zeros((units_here, width), jnp.float32),
    )
    small_zero = tuple((jnp.zeros((width,), jnp.float32) for index_slot in range(6)))

    def micro_step(totals, item):
        weight_totals, small_totals = totals
        rows_in, rows_grad, seq_length = item
        qkv_full, qkv_shift, dense_full, fc1_full, fc1_shift, fc2_full = current_set()
        residual = rows_in.astype(jnp.float32)
        normed_one, unit_one, scale_one = normalize(residual, gain_one, shift_one)
        normed_two = unit_one * gain_two + shift_two
        full_one, full_two = (
            lax.all_gather(normed_one.astype(jnp.bfloat16), "tensor", axis=0, tiled=True),
            lax.all_gather(normed_two.astype(jnp.bfloat16), "tensor", axis=0, tiled=True),
        )
        projected = jnp.einsum(
            "ld,dhe->lhe", full_one, qkv_full, preferred_element_type=jnp.float32
        ) + qkv_shift.astype(jnp.float32)
        queries = rotate(projected[..., :HD], cosines, sines).astype(jnp.bfloat16)
        key_rows = rotate(projected[..., HD : 2 * HD], cosines, sines).astype(jnp.bfloat16)
        value_rows = projected[..., 2 * HD :].astype(jnp.bfloat16)

        def mask_for(row_start):
            q_pos = lax.dynamic_slice_in_dim(positions, row_start, block_rows, 0)
            return (positions[None, :] <= q_pos[:, None]) & (positions[None, :] < seq_length)

        def attend(row_start):
            q_block = lax.dynamic_slice_in_dim(queries, row_start, block_rows, 0)
            scores = (
                jnp.einsum("qhe,khe->hqk", q_block, key_rows, preferred_element_type=jnp.float32)
                * scale
            )
            scores = jnp.where(mask_for(row_start)[None], scores, NEG_FILL)
            row_max = jnp.max(scores, axis=-1, keepdims=True)
            expo = jnp.exp(scores - row_max)
            row_sum = jnp.sum(expo, axis=-1, keepdims=True)
            softmax_w = (expo / row_sum).astype(jnp.bfloat16)
            mixed_block = jnp.einsum(
                "hqk,khe->qhe", softmax_w, value_rows, preferred_element_type=jnp.float32
            ).astype(jnp.bfloat16)
            return (mixed_block, (row_max + jnp.log(row_sum))[..., 0])

        mixed_blocks, lse_blocks = lax.map(attend, starts)
        mixed = mixed_blocks.reshape(seq_rows, heads_here, HD)
        attn_part = jnp.einsum("lhe,hed->ld", mixed, dense_full, preferred_element_type=jnp.float32)
        preact = jnp.dot(
            full_two, fc1_full, preferred_element_type=jnp.float32
        ) + fc1_shift.reshape(-1).astype(jnp.float32)
        activation = jax.nn.gelu(preact, approximate=False).astype(jnp.bfloat16)
        ffn_part = jnp.dot(activation, fc2_full, preferred_element_type=jnp.float32)
        branch = lax.psum_scatter(attn_part + ffn_part, "tensor", scatter_dimension=0, tiled=True)
        output_rows = (residual + branch + dense_shift + fc2_shift).astype(jnp.bfloat16)
        back_set = current_set()
        grad_full = lax.all_gather(rows_grad, "tensor", axis=0, tiled=True)
        grad_dense = jnp.einsum("lhe,ld->hed", mixed, grad_full, preferred_element_type=jnp.float32)
        grad_mixed = jnp.einsum(
            "ld,hed->lhe", grad_full, back_set[2], preferred_element_type=jnp.float32
        ).astype(jnp.bfloat16)
        grad_fc2 = jnp.einsum(
            "lf,ld->fd", activation, grad_full, preferred_element_type=jnp.float32
        )
        grad_act = jnp.einsum(
            "ld,fd->lf", grad_full, back_set[5], preferred_element_type=jnp.float32
        )
        normal_cdf = 0.5 * (1.0 + lax.erf(preact * SQRT_HALF))
        slope = normal_cdf + preact * jnp.exp(-0.5 * preact * preact) * INV_ROOT_TWO_PI
        grad_pre = (grad_act * slope).astype(jnp.bfloat16)
        grad_fc1 = jnp.einsum("ld,lf->df", full_two, grad_pre, preferred_element_type=jnp.float32)
        grad_fc1b = jnp.sum(grad_pre.astype(jnp.float32), axis=0).reshape(
            heads_here, units_here // heads_here
        )
        grad_second = jnp.einsum(
            "lf,df->ld", grad_pre, back_set[3], preferred_element_type=jnp.float32
        )

        def back_block(carry, block_item):
            key_grad, value_grad = carry
            row_start, lse_block = block_item
            q_block = lax.dynamic_slice_in_dim(queries, row_start, block_rows, 0)
            grad_block = lax.dynamic_slice_in_dim(grad_mixed, row_start, block_rows, 0)
            scores = (
                jnp.einsum("qhe,khe->hqk", q_block, key_rows, preferred_element_type=jnp.float32)
                * scale
            )
            scores = jnp.where(mask_for(row_start)[None], scores, NEG_FILL)
            softmax_f = jnp.exp(scores - lse_block[..., None])
            softmax_w = softmax_f.astype(jnp.bfloat16)
            value_grad = value_grad + jnp.einsum(
                "hqk,qhe->khe", softmax_w, grad_block, preferred_element_type=jnp.float32
            )
            grad_soft = jnp.einsum(
                "qhe,khe->hqk", grad_block, value_rows, preferred_element_type=jnp.float32
            )
            grad_scores = (
                softmax_f * (grad_soft - jnp.sum(softmax_f * grad_soft, axis=-1, keepdims=True))
            ).astype(jnp.bfloat16)
            query_part = (
                jnp.einsum(
                    "hqk,khe->qhe", grad_scores, key_rows, preferred_element_type=jnp.float32
                )
                * scale
            )
            key_grad = (
                key_grad
                + jnp.einsum(
                    "hqk,qhe->khe", grad_scores, q_block, preferred_element_type=jnp.float32
                )
                * scale
            )
            return ((key_grad, value_grad), query_part)

        zero_heads = jnp.zeros((seq_rows, heads_here, HD), jnp.float32)
        (key_grad, value_grad), query_parts = lax.scan(
            back_block, (zero_heads, zero_heads), (starts, lse_blocks)
        )
        query_grad = query_parts.reshape(seq_rows, heads_here, HD)
        grad_qkv = jnp.concatenate(
            [rotate(query_grad, cosines, -sines), rotate(key_grad, cosines, -sines), value_grad],
            axis=-1,
        ).astype(jnp.bfloat16)
        grad_qkvw = jnp.einsum(
            "ld,lhe->dhe", full_one, grad_qkv, preferred_element_type=jnp.float32
        )
        grad_qkvb = jnp.sum(grad_qkv.astype(jnp.float32), axis=0)
        grad_first = jnp.einsum(
            "lhe,dhe->ld", grad_qkv, back_set[0], preferred_element_type=jnp.float32
        )
        upstream = rows_grad.astype(jnp.float32)
        upstream_sum = jnp.sum(upstream, axis=0)
        norm_one, norm_two = (
            lax.psum_scatter(grad_first, "tensor", scatter_dimension=0, tiled=True),
            lax.psum_scatter(grad_second, "tensor", scatter_dimension=0, tiled=True),
        )
        input_rows = (
            upstream
            + norm_back(norm_one, unit_one, scale_one, gain_one)
            + norm_back(norm_two, unit_one, scale_one, gain_two)
        ).astype(jnp.bfloat16)
        small_terms = (
            jnp.sum(norm_one * unit_one, axis=0),
            jnp.sum(norm_one, axis=0),
            jnp.sum(norm_two * unit_one, axis=0),
            jnp.sum(norm_two, axis=0),
            upstream_sum,
            upstream_sum,
        )
        weight_terms = (grad_qkvw, grad_qkvb, grad_dense, grad_fc1, grad_fc1b, grad_fc2)
        new_weights = tuple((total + term for total, term in zip(weight_totals, weight_terms)))
        new_small = tuple((total + term for total, term in zip(small_totals, small_terms)))
        return ((new_weights, new_small), (output_rows, input_rows))

    (weight_totals, small_totals), (output_rows, input_rows) = lax.scan(
        micro_step, (weight_zero, small_zero), (got_in[:, 0], got_grad[:, 0], my_lengths)
    )
    weight_sums = (
        lax.psum_scatter(
            weight_totals[0].astype(jnp.bfloat16), "dp", scatter_dimension=0, tiled=True
        ).astype(jnp.float32),
        lax.psum_scatter(
            weight_totals[1].astype(jnp.bfloat16), "dp", scatter_dimension=1, tiled=True
        ).astype(jnp.float32),
        lax.psum_scatter(
            weight_totals[2].astype(jnp.bfloat16), "dp", scatter_dimension=1, tiled=True
        ).astype(jnp.float32),
        lax.psum_scatter(
            weight_totals[3].astype(jnp.bfloat16), "dp", scatter_dimension=0, tiled=True
        ).astype(jnp.float32),
        lax.psum_scatter(
            weight_totals[4].astype(jnp.bfloat16), "dp", scatter_dimension=1, tiled=True
        ).astype(jnp.float32),
        lax.psum_scatter(
            weight_totals[5].astype(jnp.bfloat16), "dp", scatter_dimension=1, tiled=True
        ).astype(jnp.float32),
    )
    small_sums = lax.psum_scatter(small_totals, ("dp", "tensor"), scatter_dimension=0, tiled=True)
    back_out, back_grad = (
        lax.all_to_all(output_rows[:, None], "dp", split_axis=2, concat_axis=1, tiled=True),
        lax.all_to_all(input_rows[:, None], "dp", split_axis=2, concat_axis=1, tiled=True),
    )
    slot_ids = jnp.arange(seq_count, dtype=jnp.int32)
    inverse = jnp.sum(
        jnp.where(dealing[:, :, None] == slot_ids[None, None, :], slot_ids[None, :, None], 0),
        axis=1,
    )
    output = jax.vmap(take_slots)(back_out, inverse)
    input_grad = jax.vmap(take_slots)(back_grad, inverse)
    return (
        output,
        input_grad,
        small_sums[0],
        small_sums[1],
        small_sums[2],
        small_sums[3],
        weight_sums[0],
        weight_sums[1],
        weight_sums[2],
        small_sums[4],
        weight_sums[3],
        weight_sums[4],
        weight_sums[5],
        small_sums[5],
    )


def solution(mesh):
    return jax.shard_map(
        per_device,
        mesh=mesh,
        in_specs=(
            P(None, None, ("dp", "tensor"), None),
            P(),
            P(),
            P(None, None, ("dp", "tensor"), None),
            P(("dp", "tensor")),
            P(("dp", "tensor")),
            P(("dp", "tensor")),
            P(("dp", "tensor")),
            P("dp", "tensor", None),
            P("tensor", "dp"),
            P("tensor", "dp", None),
            P(("dp", "tensor")),
            P("dp", "tensor"),
            P("tensor", "dp"),
            P("tensor", "dp"),
            P(("dp", "tensor")),
        ),
        out_specs=(
            P(None, None, ("dp", "tensor"), None),
            P(None, None, ("dp", "tensor"), None),
            P(("dp", "tensor")),
            P(("dp", "tensor")),
            P(("dp", "tensor")),
            P(("dp", "tensor")),
            P("dp", "tensor", None),
            P("tensor", "dp"),
            P("tensor", "dp", None),
            P(("dp", "tensor")),
            P("dp", "tensor"),
            P("tensor", "dp"),
            P("tensor", "dp"),
            P(("dp", "tensor")),
        ),
        check_vma=False,
    )
```

profile of v0, /device:TPU:0, one launch (start us, length us, event | category | flops | bytes accessed | tf_op | source)
XLA Modules:
  0.0 2300.3 jit_solution(938326112984021490)
XLA Ops:
  28.8 23.3 %all-to-all-done = bf16[2,8,32,2048]{3,2,0,1:T(8,128)(2,1)S(1)} async-done(((bf16[2,8,32,2048]{3,2,0,1:T(8,128)(2,1)}), bf16[2,8,32,2048]{3,2,0,1:T(8,128)(2,1)S(1)}, u32[]{:S(2)}, u32[]{:S(2)}) %all-to-all-start) | async-done | bytes 2097184 | tf_op jit(solution)/shard_map/all_to_all | solution.py:88
  58.2 58.6 %all-reduce.14 = (bf16[2048]{0:T(1024)(128)(2,1)S(1)}, bf16[2048]{0:T(1024)(128)(2,1)S(1)}, bf16[2048]{0:T(1024)(128)(2,1)S(1)}, bf16[2048]{0:T(1024)(128)(2,1)S...) all-reduce(bf16[2048]{0:T(1024)(128)(2,1)S(1)} %dynamic-update-slic, ...), channel_id=1, replica_groups=mesh['dp'=8,'tensor'=4] {'dp','tensor'}, use_global_device_ids=true, to_apply=%add | all-reduce | flops 12288 | bytes 49152
  127.4 1772.7 %while.89 = (s32[]{:T(128)}, f32[2048,2,768]{2,0,1:T(8,128)}, f32[2,768]{1,0:T(2,128)}, f32[2,256,2048]{2,1,0:T(8,128)}, f32[2048,2048]{1,0:T(8,128)}, /*index=5...) while((s32[]{:T(128)}, f32[2048,2,768]{2,0,1:T(8,128)}, ...), condition=%wide.region_24.26_spmd.clone.clone.clone.clone, body=%wide.region_0.25_spmd.clone.clone.clone.clone.sunk | while | flops 81338195968 | bytes 859343296 | solution.py:280
  157.5 82.4 %all-gather.26.cloned.1.call-done = bf16[1,1024,2048]{2,1,0:T(8,128)(2,1)} async-done(((bf16[1,256,2048]{2,1,0:T(8,128)(2,1)}), bf16[1,1024,2048]{2,1,0:T(8,128)(2,1)}) %all-gather.26.cloned.1.call-update) | async-done | bytes 4194320 | tf_op jit(solution)/shard_map/while/body/eval_jaxpr/all_gather | solution.py:182
  246.1 74.7 %all-gather.22.cloned.1.call-done = bf16[1024,2048]{1,0:T(8,128)(2,1)} async-done(((bf16[256,2048]{1,0:T(8,128)(2,1)}), bf16[1024,2048]{1,0:T(8,128)(2,1)}) %all-gather.22.cloned.1.call-update) | async-done | bytes 4194320 | tf_op jit(solution)/shard_map/while/body/eval_jaxpr/all_gather | solution.py:141
  320.8 47.0 %all-gather.20.cloned.1.call-done = bf16[2048,2,768]{0,2,1:T(8,128)(2,1)} async-done(((bf16[256,2,768]{0,2,1:T(8,128)(2,1)}), bf16[2048,2,768]{0,2,1:T(8,128)(2,1)}) %all-gather.20.cloned.1.call-update) | async-done | bytes 6291472 | tf_op jit(solution)/shard_map/while/body/eval_jaxpr/all_gather | solution.py:106
  386.6 17.4 while.90
  405.0 87.3 %while.91 = (s32[]{:T(128)}, f32[1024,2,256]{0,2,1:T(8,128)}, f32[1024,2,256]{0,2,1:T(8,128)}, f32[2,512,2,256]{1,0,3,2:T(2,128)}, s32[2]{0:T(128)S(1)}, /*index...) while((s32[]{:T(128)}, f32[1024,2,256]{0,2,1:T(8,128)}, ...), condition=%wide.region_9.10_spmd.clone.clone, body=%wide.region_7.9_spmd.clone.clone.sunk | while | flops 2704015360 | bytes 111194568 | solution.py:241
  421.3 19.6 dynamic_update_slice.44
  463.7 19.6 dynamic_update_slice.44
  538.0 31.3 %fusion.250 = (bf16[1024,2048]{1,0:T(8,128)(2,1)}, f32[1024,2048]{1,0:T(8,128)}) fusion(f32[2048]{0:T(1024)S(1)} %bitcast.334, bf16[1024,2048]{1,0:T(8,128)(2,1)} %all-gather.28.cloned.1.call-done, bf16[2048,2048]{1,0:T(8,128)(2,1)} %all-gather.30.cloned.1.call-done), kind=kOutput, calls=%fused_computation.67.clone.1 | convolution fusion | flops 8728346624 | bytes 25174016 | tf_op jit(solution)/shard_map/while/body/eval_jaxpr/dot_general | solution.py:174
  665.1 44.9 %reduce-scatter.25.cloned.1.call-done = f32[256,2048]{1,0:T(8,128)} async-done(((f32[1024,2048]{1,0:T(8,128)}), f32[256,2048]{1,0:T(8,128)}) %reduce-scatter.25.cloned.1.call-update) | async-done | bytes 2097168 | tf_op jit(solution)/shard_map/while/body/eval_jaxpr/reduce_scatter | solution.py:259
  710.0 147.6 %reduce-scatter.23.cloned.1.call-done = f32[256,2048]{1,0:T(8,128)} async-done(((f32[1024,2048]{1,0:T(8,128)}), f32[256,2048]{1,0:T(8,128)}) %reduce-scatter.23.cloned.1.call-update) | async-done | bytes 2097168 | tf_op jit(solution)/shard_map/while/body/eval_jaxpr/reduce_scatter | solution.py:260
  861.8 143.2 %reduce-scatter.27.cloned.1.call-done = f32[256,2048]{1,0:T(8,128)} async-done(((f32[1024,2048]{1,0:T(8,128)}), f32[256,2048]{1,0:T(8,128)}) %reduce-scatter.27.cloned.1.call-update) | async-done | bytes 2097168 | tf_op jit(solution)/shard_map/while/body/eval_jaxpr/reduce_scatter | solution.py:179
  1041.8 82.2 %all-gather.26.cloned.1.call-done = bf16[1,1024,2048]{2,1,0:T(8,128)(2,1)} async-done(((bf16[1,256,2048]{2,1,0:T(8,128)(2,1)}), bf16[1,1024,2048]{2,1,0:T(8,128)(2,1)}) %all-gather.26.cloned.1.call-update) | async-done | bytes 4194320 | tf_op jit(solution)/shard_map/while/body/eval_jaxpr/all_gather | solution.py:182
  1130.2 74.7 %all-gather.22.cloned.1.call-done = bf16[1024,2048]{1,0:T(8,128)(2,1)} async-done(((bf16[256,2048]{1,0:T(8,128)(2,1)}), bf16[1024,2048]{1,0:T(8,128)(2,1)}) %all-gather.22.cloned.1.call-update) | async-done | bytes 4194320 | tf_op jit(solution)/shard_map/while/body/eval_jaxpr/all_gather | solution.py:141
  1204.9 47.0 %all-gather.20.cloned.1.call-done = bf16[2048,2,768]{0,2,1:T(8,128)(2,1)} async-done(((bf16[256,2,768]{0,2,1:T(8,128)(2,1)}), bf16[2048,2,768]{0,2,1:T(8,128)(2,1)}) %all-gather.20.cloned.1.call-update) | async-done | bytes 6291472 | tf_op jit(solution)/shard_map/while/body/eval_jaxpr/all_gather | solution.py:106
  1270.8 17.4 while.90
  1289.2 87.3 %while.91 = (s32[]{:T(128)}, f32[1024,2,256]{0,2,1:T(8,128)}, f32[1024,2,256]{0,2,1:T(8,128)}, f32[2,512,2,256]{1,0,3,2:T(2,128)}, s32[2]{0:T(128)S(1)}, /*index...) while((s32[]{:T(128)}, f32[1024,2,256]{0,2,1:T(8,128)}, ...), condition=%wide.region_9.10_spmd.clone.clone, body=%wide.region_7.9_spmd.clone.clone.sunk | while | flops 2704015360 | bytes 111194568 | solution.py:241
  1305.5 19.6 dynamic_update_slice.44
  1347.9 19.6 dynamic_update_slice.44
  1422.2 31.4 %fusion.250 = (bf16[1024,2048]{1,0:T(8,128)(2,1)}, f32[1024,2048]{1,0:T(8,128)}) fusion(f32[2048]{0:T(1024)S(1)} %bitcast.334, bf16[1024,2048]{1,0:T(8,128)(2,1)} %all-gather.28.cloned.1.call-done, bf16[2048,2048]{1,0:T(8,128)(2,1)} %all-gather.30.cloned.1.call-done), kind=kOutput, calls=%fused_computation.67.clone.1 | convolution fusion | flops 8728346624 | bytes 25174016 | tf_op jit(solution)/shard_map/while/body/eval_jaxpr/dot_general | solution.py:174
  1524.7 18.5 select_add_fusion.24
  1559.4 34.4 %reduce-scatter.25.cloned.1.call-done = f32[256,2048]{1,0:T(8,128)} async-done(((f32[1024,2048]{1,0:T(8,128)}), f32[256,2048]{1,0:T(8,128)}) %reduce-scatter.25.cloned.1.call-update) | async-done | bytes 2097168 | tf_op jit(solution)/shard_map/while/body/eval_jaxpr/reduce_scatter | solution.py:259
  1593.8 147.6 %reduce-scatter.23.cloned.1.call-done = f32[256,2048]{1,0:T(8,128)} async-done(((f32[1024,2048]{1,0:T(8,128)}), f32[256,2048]{1,0:T(8,128)}) %reduce-scatter.23.cloned.1.call-update) | async-done | bytes 2097168 | tf_op jit(solution)/shard_map/while/body/eval_jaxpr/reduce_scatter | solution.py:260
  1745.6 143.2 %reduce-scatter.27.cloned.1.call-done = f32[256,2048]{1,0:T(8,128)} async-done(((f32[1024,2048]{1,0:T(8,128)}), f32[256,2048]{1,0:T(8,128)}) %reduce-scatter.27.cloned.1.call-update) | async-done | bytes 2097168 | tf_op jit(solution)/shard_map/while/body/eval_jaxpr/reduce_scatter | solution.py:179
  1907.4 21.9 copy.230
  1961.7 22.5 all-to-all-done.3
  1990.1 64.1 %all-reduce.13 = (f32[2048]{0:T(1024)S(1)}, f32[2048]{0:T(1024)S(1)}, f32[2048]{0:T(1024)S(1)}, f32[2048]{0:T(1024)S(1)}, f32[2048]{0:T(1024)S(1)}, /*index=5*/f32[2048]{0:T(1024)S(1)}) all-reduce(f32[2048]{0:T(1024)S(1)} %copy-done.33, f32[2048]{0:T(1024)S(1)} %copy-done.36, ...), channel_id=6, replica_groups=mesh['dp'=8,'tensor'=4] {'dp','tensor'}, use_global_device_ids=true, to_apply=%region_26.28.clone | all-reduce | flops 12288 | bytes 98304
  2077.5 62.7 %all-reduce.17.cloned.1.call-done = bf16[2048,2,768]{2,1,0:T(2,128)(2,1)} async-done(((bf16[2048,2,768]{2,1,0:T(2,128)(2,1)}), bf16[2048,2,768]{2,1,0:T(2,128)(2,1)}) %all-reduce.17.cloned.1.call-update) | async-done | bytes 6291472
  2143.0 72.0 %reduce-scatter.15.cloned.1.call-done = bf16[256,2048]{1,0:T(8,128)(2,1)} async-done(((bf16[2048,2048]{1,0:T(8,128)(2,1)}), bf16[256,2048]{1,0:T(8,128)(2,1)}) %reduce-scatter.15.cloned.1.call-update) | async-done | bytes 1048592 | tf_op jit(solution)/shard_map/reduce_scatter | solution.py:293
  2217.7 72.2 %reduce-scatter.17.cloned.1.call-done = bf16[2048,256]{1,0:T(8,128)(2,1)} async-done(((bf16[2048,2048]{1,0:T(8,128)(2,1)}), bf16[2048,256]{1,0:T(8,128)(2,1)}) %reduce-scatter.17.cloned.1.call-update) | async-done | bytes 1048592 | tf_op jit(solution)/shard_map/reduce_scatter | solution.py:299
  (635 shorter events, 632.4 us)
Async XLA Ops:
  20.3 31.8 %all-to-all-start = ((bf16[2,8,32,2048]{3,2,0,1:T(8,128)(2,1)}), bf16[2,8,32,2048]{3,2,0,1:T(8,128)(2,1)S(1)}, u32[]{:S(2)}, u32[]{:S(2)}) async-start(bf16[2,8,32,2048]{3,2,0,1:T(8,128)(2,1)} %copy.186), calls=%async_computation.3 | async-start | bytes 4194304 | tf_op jit(solution)/shard_map/all_to_all | solution.py:88
  52.1 72.2 %all-to-all-start.1 = ((bf16[2,8,32,2048]{3,2,0,1:T(8,128)(2,1)}), bf16[2,8,32,2048]{3,2,0,1:T(8,128)(2,1)}, u32[]{:S(2)}, u32[]{:S(2)}) async-start(bf16[2,8,32,2048]{3,2,0,1:T(8,128)(2,1)} %copy.188), calls=%async_computation.4 | async-start | bytes 4194304 | tf_op jit(solution)/shard_map/all_to_all | solution.py:89
  127.8 29.7 %all-gather.24.cloned.1.call-start = ((), (), s32[]{:S(2)}) async-start(), calls=%async_computation.20 | async-start | bytes 2359296 | tf_op jit(solution)/shard_map/while/body/eval_jaxpr/all_gather | solution.py:108
  128.5 111.3 %all-gather.26.cloned.1.call-start = ((), (), s32[]{:S(2)}) async-start(), calls=%async_computation.21 | async-start | bytes 5242880 | tf_op jit(solution)/shard_map/while/body/eval_jaxpr/all_gather | solution.py:182
  131.7 189.1 %all-gather.22.cloned.1.call-start = ((), (), s32[]{:S(2)}) async-start(), calls=%async_computation.19 | async-start | bytes 5242880 | tf_op jit(solution)/shard_map/while/body/eval_jaxpr/all_gather | solution.py:141
  135.4 232.4 %all-gather.20.cloned.1.call-start = ((), (), s32[]{:S(2)}) async-start(), calls=%async_computation.18 | async-start | bytes 7077888 | tf_op jit(solution)/shard_map/while/body/eval_jaxpr/all_gather | solution.py:106
  135.9 402.0 %all-gather.28.cloned.1.call-start = ((), (), s32[]{:S(2)}) async-start(), calls=%async_computation.22 | async-start | bytes 5242880 | tf_op jit(solution)/shard_map/while/body/eval_jaxpr/all_gather | solution.py:142
  136.5 401.5 %all-gather.30.cloned.1.call-start = ((), (), s32[]{:S(2)}) async-start(), calls=%async_computation.23 | async-start | bytes 9437184 | tf_op jit(solution)/shard_map/while/body/eval_jaxpr/all_gather | solution.py:109
  137.1 432.2 %all-gather.32.cloned.1.call-start = ((), (), s32[]{:S(2)}) async-start(), calls=%async_computation.24 | async-start | bytes 9437184 | tf_op jit(solution)/shard_map/while/body/eval_jaxpr/all_gather | solution.py:111
  137.9 572.1 %reduce-scatter.25.cloned.1.call-start = ((), (), s32[]{:S(2)}) async-start(), calls=%async_computation.26 | async-start | bytes 10485760 | tf_op jit(solution)/shard_map/while/body/eval_jaxpr/reduce_scatter | solution.py:259
  528.6 329.0 %reduce-scatter.23.cloned.1.call-start = ((), (), s32[]{:S(2)}) async-start(), calls=%async_computation.25 | async-start | bytes 10485760 | tf_op jit(solution)/shard_map/while/body/eval_jaxpr/reduce_scatter | solution.py:260
  599.9 405.1 %reduce-scatter.27.cloned.1.call-start = ((), (), s32[]{:S(2)}) async-start(), calls=%async_computation.27 | async-start | bytes 10485760 | tf_op jit(solution)/shard_map/while/body/eval_jaxpr/reduce_scatter | solution.py:179
  665.0 340.0 %copy-start.13 = (bf16[1,256,2048]{2,1,0:T(8,128)(2,1)S(1)}, bf16[1,256,2048]{2,1,0:T(8,128)(2,1)}, u32[]{:S(2)}) copy-start(bf16[1,256,2048]{2,1,0:T(8,128)(2,1)} %get-tuple-element.1932) | copy-start | bytes 3145732 | tf_op jit(solution)/shard_map/while
  665.0 340.0 %copy-start.49 = (f32[2048]{0:T(1024)S(1)}, f32[2048]{0:T(1024)}, u32[]{:S(2)}) copy-start(f32[2048]{0:T(1024)} %get-tuple-element.2181) | copy-start | bytes 24580 | tf_op jit(solution)/shard_map/while
  1010.4 31.4 %all-gather.24.cloned.1.call-start = ((), (), s32[]{:S(2)}) async-start(), calls=%async_computation.20 | async-start | bytes 2359296 | tf_op jit(solution)/shard_map/while/body/eval_jaxpr/all_gather | solution.py:108
  1011.1 112.9 %all-gather.26.cloned.1.call-start = ((), (), s32[]{:S(2)}) async-start(), calls=%async_computation.21 | async-start | bytes 5242880 | tf_op jit(solution)/shard_map/while/body/eval_jaxpr/all_gather | solution.py:182
  1014.3 190.6 %all-gather.22.cloned.1.call-start = ((), (), s32[]{:S(2)}) async-start(), calls=%async_computation.19 | async-start | bytes 5242880 | tf_op jit(solution)/shard_map/while/body/eval_jaxpr/all_gather | solution.py:141
  1018.0 233.9 %all-gather.20.cloned.1.call-start = ((), (), s32[]{:S(2)}) async-start(), calls=%async_computation.18 | async-start | bytes 7077888 | tf_op jit(solution)/shard_map/while/body/eval_jaxpr/all_gather | solution.py:106
  1018.5 403.6 %all-gather.28.cloned.1.call-start = ((), (), s32[]{:S(2)}) async-start(), calls=%async_computation.22 | async-start | bytes 5242880 | tf_op jit(solution)/shard_map/while/body/eval_jaxpr/all_gather | solution.py:142
  1019.1 403.0 %all-gather.30.cloned.1.call-start = ((), (), s32[]{:S(2)}) async-start(), calls=%async_computation.23 | async-start | bytes 9437184 | tf_op jit(solution)/shard_map/while/body/eval_jaxpr/all_gather | solution.py:109
  1019.7 433.8 %all-gather.32.cloned.1.call-start = ((), (), s32[]{:S(2)}) async-start(), calls=%async_computation.24 | async-start | bytes 9437184 | tf_op jit(solution)/shard_map/while/body/eval_jaxpr/all_gather | solution.py:111
  1020.3 573.5 %reduce-scatter.25.cloned.1.call-start = ((), (), s32[]{:S(2)}) async-start(), calls=%async_computation.26 | async-start | bytes 10485760 | tf_op jit(solution)/shard_map/while/body/eval_jaxpr/reduce_scatter | solution.py:259
  1412.7 328.7 %reduce-scatter.23.cloned.1.call-start = ((), (), s32[]{:S(2)}) async-start(), calls=%async_computation.25 | async-start | bytes 10485760 | tf_op jit(solution)/shard_map/while/body/eval_jaxpr/reduce_scatter | solution.py:260
  1484.0 404.8 %reduce-scatter.27.cloned.1.call-start = ((), (), s32[]{:S(2)}) async-start(), calls=%async_computation.27 | async-start | bytes 10485760 | tf_op jit(solution)/shard_map/while/body/eval_jaxpr/reduce_scatter | solution.py:179
  1900.2 157.4 %reduce-scatter.19.cloned.1.call-start = ((), (), s32[]{:S(2)}) async-start(), calls=%async_computation.15 | async-start | bytes 221184
  1901.8 157.2 %reduce-scatter.21.cloned.1.call-start = ((), (), s32[]{:S(2)}) async-start(), calls=%async_computation.16 | async-start | bytes 294912
  1903.5 172.0 %reduce-scatter.13.cloned.1.call-start = ((), (), s32[]{:S(2)}) async-start(), calls=%async_computation.12 | async-start | bytes 2359296 | tf_op jit(solution)/shard_map/reduce_scatter | solution.py:290
  1907.4 232.8 %all-reduce.17.cloned.1.call-start = ((), (), s32[]{:S(2)}) async-start(), calls=%async_computation.17 | async-start | bytes 12582912
  1929.4 285.5 %reduce-scatter.15.cloned.1.call-start = ((), (), s32[]{:S(2)}) async-start(), calls=%async_computation.13 | async-start | bytes 9437184 | tf_op jit(solution)/shard_map/reduce_scatter | solution.py:293
  1938.6 351.4 %reduce-scatter.17.cloned.1.call-start = ((), (), s32[]{:S(2)}) async-start(), calls=%async_computation.14 | async-start | bytes 9437184 | tf_op jit(solution)/shard_map/reduce_scatter | solution.py:299
  1952.8 31.4 %all-to-all-start.3 = ((bf16[2,1,256,2048]{3,0,1,2:T(2,128)(2,1)}), bf16[2,1,256,2048]{3,0,1,2:T(2,128)(2,1)S(1)}, u32[]{:S(2)}, u32[]{:S(2)}) async-start(bf16[2,1,256,2048]{3,0,1,2:T(2,128)(2,1)} %bitcast.325), calls=%async_computation.6 | async-start | bytes 4194304 | tf_op jit(solution)/shard_map/all_to_all | solution.py:306
  1984.2 82.0 %all-to-all-start.2 = ((bf16[2,1,256,2048]{3,0,1,2:T(2,128)(2,1)}), bf16[2,1,256,2048]{3,0,1,2:T(2,128)(2,1)}, u32[]{:S(2)}, u32[]{:S(2)}) async-start(bf16[2,1,256,2048]{3,0,1,2:T(2,128)(2,1)} %bitcast.324), calls=%async_computation.5 | async-start | bytes 4194304 | tf_op jit(solution)/shard_map/all_to_all | solution.py:305
  (138 other events, 6812.9 us)
Sparse Core Ops, SparseCore 0:
  130.6 26.9 all-gather.23
  159.1 80.7 all-gather.25
  241.5 79.2 all-gather.21
  322.5 45.1 all-gather.19
  369.7 80.7 all-gather.27
  452.3 52.9 all-gather.29
  507.1 55.9 all-gather.31
  565.5 144.4 reduce-scatter.24
  712.3 145.1 reduce-scatter.22
  859.8 145.1 reduce-scatter.26
  1013.1 28.6 all-gather.23
  1043.2 80.7 all-gather.25
  1125.6 79.2 all-gather.21
  1206.7 45.1 all-gather.19
  1253.9 80.7 all-gather.27
  1336.4 52.9 all-gather.29
  1391.1 55.9 all-gather.31
  1449.3 144.4 reduce-scatter.24
  1596.2 145.1 reduce-scatter.22
  1743.6 145.1 reduce-scatter.26
Sparse Core Ops, SparseCore 1:
  1904.2 34.2 reduce-scatter.18
  1942.3 34.7 reduce-scatter.20
  1980.2 51.9 reduce-scatter.12
  2035.8 104.3 all-reduce.16
  2143.6 71.2 reduce-scatter.14
  2218.8 71.1 reduce-scatter.16
where the time goes:
time: 2310 us; the launch traced here: 2300 us
  waiting for transfers between devices  1340 us (58%)
  matrix products  387 us (17%)
  local copies, waits for them, and re-layouts  238 us (10%)
  blocking collectives  159 us (7%)
  other arithmetic  111 us (5%)
  loops' own time  25.3 us (1%)
    reduce_scatter x2, waiting for transfers between devices, micro_step(): lax.psum_scatter(grad_second, 'tensor', scatter_dimension=0, tiled=True)  295 us
    reduce_scatter x2, waiting for transfers between devices, micro_step(): lax.psum_scatter(attn_part + ffn_part, 'tensor', scatter_dimension=0, til...  286 us
    all_gather x2, waiting for transfers between devices, micro_step(): grad_full = lax.all_gather(rows_grad, 'tensor', axis=0, tiled=True)  165 us
    all_gather x2, waiting for transfers between devices, micro_step(): lax.all_gather(normed_one.astype(jnp.bfloat16), 'tensor', axis=0, tiled=T...  149 us
    unnamed x2, blocking collectives  123 us
    all_gather x2, waiting for transfers between devices, current_set(): lax.all_gather(shard_set[0], 'dp', axis=0, tiled=True)  93.9 us
    dynamic_update_slice x8, local copies, waits for them, and re-layouts, micro_step(): lax.scan(back_block, (zero_heads, zero_heads), (starts, lse_blocks))  92.7 us
    reduce_scatter x2, waiting for transfers between devices, micro_step(): lax.psum_scatter(grad_first, 'tensor', scatter_dimension=0, tiled=True)  79.3 us
  transfers between devices with their start and end apart: 30, of which 19 were waited for; matrix products, arithmetic and copies ran while one was open for 30% of the time, Pallas kernels for 0%

commit v1 on v0

--- a/solution.py
+++ b/solution.py
@@ -179,7 +179,14 @@
         branch = lax.psum_scatter(attn_part + ffn_part, "tensor", scatter_dimension=0, tiled=True)
         output_rows = (residual + branch + dense_shift + fc2_shift).astype(jnp.bfloat16)
         back_set = current_set()
-        grad_full = lax.all_gather(rows_grad, "tensor", axis=0, tiled=True)
+        devices = lax.axis_size("tensor")
+        hops = [(i, (i + 1) % devices) for i in range(devices)]
+        blocks = [rows_grad]
+        for hop in range(1, devices):
+            blocks = [lax.ppermute(blocks[0], "tensor", hops), *blocks]
+        whole = jnp.concatenate(blocks, axis=0)
+        offset = (lax.axis_index("tensor") + 1) * blocks[-1].shape[0]
+        grad_full = jnp.roll(whole, offset, axis=0)
         grad_dense = jnp.einsum("lhe,ld->hed", mixed, grad_full, preferred_element_type=jnp.float32)
         grad_mixed = jnp.einsum(
             "ld,hed->lhe", grad_full, back_set[2], preferred_element_type=jnp.float32

time: 2310 us -> 2230 us (0.965)
  waiting for transfers between devices: 1340 us -> 1200 us
  starting transfers between devices: 18.6 us -> 45.9 us
  local copies, waits for them, and re-layouts: 238 us -> 262 us
    ppermute x0 -> x6, waiting for transfers between devices: none -> 214 us  [micro_step(): blocks = [lax.ppermute(blocks[0], 'tensor', hops), *blocks]]
    all_gather x2 -> x0, waiting for transfers between devices: 165 us -> none  [micro_step(): grad_full = lax.all_gather(rows_grad, 'tensor', axis=0, tiled=True)]
    all_gather x2, waiting for transfers between devices: 149 us -> 0.01 us  [micro_step(): lax.all_gather(normed_one.astype(jnp.bfloat16), 'tensor', axis=0, tiled=T...]
    ppermute x0 -> x6, starting transfers between devices: none -> 27.4 us  [micro_step(): blocks = [lax.ppermute(blocks[0], 'tensor', hops), *blocks]]
    all_gather x2, waiting for transfers between devices: 93.9 us -> 70.3 us  [current_set(): lax.all_gather(shard_set[0], 'dp', axis=0, tiled=True)]
  transfers between devices with their start and end apart: 30 -> 34, of which waited for: 19 -> 19; matrix products, arithmetic and copies ran while one was open for 30% -> 33% of each run, Pallas kernels for 0% -> 0%
where the time goes in v1:
time: 2230 us; the launch traced here: 2220 us
  waiting for transfers between devices  1200 us (54%)
  matrix products  395 us (18%)
  local copies, waits for them, and re-layouts  262 us (12%)
  blocking collectives  157 us (7%)
  other arithmetic  116 us (5%)
  starting transfers between devices  45.9 us (2%)
  loops' own time  24.8 us (1%)
    reduce_scatter x2, waiting for transfers between devices, micro_step(): lax.psum_scatter(grad_second, 'tensor', scatter_dimension=0, tiled=True)  295 us
    reduce_scatter x2, waiting for transfers between devices, micro_step(): lax.psum_scatter(attn_part + ffn_part, 'tensor', scatter_dimension=0, til...  286 us
    ppermute x6, waiting for transfers between devices, micro_step(): blocks = [lax.ppermute(blocks[0], 'tensor', hops), *blocks]  214 us
    unnamed x2, blocking collectives  123 us
    dynamic_update_slice x8, local copies, waits for them, and re-layouts, micro_step(): lax.scan(back_block, (zero_heads, zero_heads), (starts, lse_blocks))  93 us
    reduce_scatter x2, waiting for transfers between devices, micro_step(): lax.psum_scatter(grad_first, 'tensor', scatter_dimension=0, tiled=True)  75.4 us
    reduce_scatter x1, waiting for transfers between devices, per_device(): lax.psum_scatter(weight_totals[5].astype(jnp.bfloat16), 'dp', scatter_dim...  72.2 us
    reduce_scatter x1, waiting for transfers between devices, per_device(): lax.psum_scatter(weight_totals[3].astype(jnp.bfloat16), 'dp', scatter_dim...  72 us
  transfers between devices with their start and end apart: 34, of which 19 were waited for; matrix products, arithmetic and copies ran while one was open for 33% of the time, Pallas kernels for 0%

profile of v1, /device:TPU:0, one launch (start us, length us, event | category | flops | bytes accessed | tf_op | source)
XLA Modules:
  0.0 2217.5 jit_solution(5620455461615828725)
XLA Ops:
  28.8 23.3 %all-to-all-done = bf16[2,8,32,2048]{3,2,0,1:T(8,128)(2,1)S(1)} async-done(((bf16[2,8,32,2048]{3,2,0,1:T(8,128)(2,1)}), bf16[2,8,32,2048]{3,2,0,1:T(8,128)(2,1)S(1)}, u32[]{:S(2)}, u32[]{:S(2)}) %all-to-all-start) | async-done | bytes 2097184 | tf_op jit(solution)/shard_map/all_to_all | solution.py:88
  58.2 58.6 %all-reduce.14 = (bf16[2048]{0:T(1024)(128)(2,1)S(1)}, bf16[2048]{0:T(1024)(128)(2,1)S(1)}, bf16[2048]{0:T(1024)(128)(2,1)S(1)}, bf16[2048]{0:T(1024)(128)(2,1)S...) all-reduce(bf16[2048]{0:T(1024)(128)(2,1)S(1)} %dynamic-update-slic, ...), channel_id=1, replica_groups=mesh['dp'=8,'tensor'=4] {'dp','tensor'}, use_global_device_ids=true, to_apply=%add | all-reduce | flops 12288 | bytes 49152
  127.6 1689.7 %while.108 = (s32[]{:T(128)}, f32[2048,2,768]{2,0,1:T(8,128)}, f32[2,768]{1,0:T(2,128)}, f32[2,256,2048]{2,1,0:T(8,128)}, f32[2048,2048]{1,0:T(8,128)}, /*index=...) while((s32[]{:T(128)}, f32[2048,2,768]{2,0,1:T(8,128)}, ...), condition=%wide.region_24.26_spmd.clone.clone.clone.clone, body=%wide.region_0.25_spmd.clone.clone.clone.clone.sunk | while | flops 81338195968 | bytes 852526464 | solution.py:287
  139.3 25.5 %collective-permute-done = bf16[256,2048]{1,0:T(8,128)(2,1)S(1)} collective-permute-done((bf16[256,2048]{1,0:T(8,128)(2,1)S(1)}, bf16[256,2048]{1,0:T(8,128)(2,1)S(1)}, u32[]{:S(2)}, u32[]{:S(2)}) %collective-permute-start) | collective-permute-done | bytes 1048608 | tf_op jit(solution)/shard_map/while/body/eval_jaxpr/ppermute | solution.py:186
  164.9 46.1 %collective-permute-done.1 = bf16[256,2048]{1,0:T(8,128)(2,1)} collective-permute-done((bf16[256,2048]{1,0:T(8,128)(2,1)S(1)}, bf16[256,2048]{1,0:T(8,128)(2,1)}, u32[]{:S(2)}, u32[]{:S(2)}) %collective-permute-start.1) | collective-permute-done | bytes 1048608 | tf_op jit(solution)/shard_map/while/body/eval_jaxpr/ppermute | solution.py:186
  230.6 40.7 %collective-permute-done.2 = bf16[256,2048]{1,0:T(8,128)(2,1)} collective-permute-done((bf16[256,2048]{1,0:T(8,128)(2,1)}, bf16[256,2048]{1,0:T(8,128)(2,1)}, u32[]{:S(2)}, u32[]{:S(2)}) %collective-permute-start.2) | collective-permute-done | bytes 1048608 | tf_op jit(solution)/shard_map/while/body/eval_jaxpr/ppermute | solution.py:186
  291.3 35.7 %all-gather.13.cloned.1.call-done = bf16[2048,2,768]{0,2,1:T(8,128)(2,1)} async-done(((bf16[256,2,768]{0,2,1:T(8,128)(2,1)}), bf16[2048,2,768]{0,2,1:T(8,128)(2,1)}) %all-gather.13.cloned.1.call-update) | async-done | bytes 6291472 | tf_op jit(solution)/shard_map/while/body/eval_jaxpr/all_gather | solution.py:106
  364.3 87.9 %while.110 = (s32[]{:T(128)}, f32[1024,2,256]{0,2,1:T(8,128)}, f32[1024,2,256]{0,2,1:T(8,128)}, f32[2,512,2,256]{1,0,3,2:T(2,128)}, s32[2]{0:T(128)S(1)}, /*inde...) while((s32[]{:T(128)}, f32[1024,2,256]{0,2,1:T(8,128)}, ...), condition=%wide.region_9.10_spmd.clone.clone, body=%wide.region_7.9_spmd.clone.clone.sunk | while | flops 2704015360 | bytes 111194568 | solution.py:248
  380.9 19.7 dynamic_update_slice.48
  423.4 19.7 dynamic_update_slice.48
  497.9 31.2 %fusion.255 = (bf16[1024,2048]{1,0:T(8,128)(2,1)}, f32[1024,2048]{1,0:T(8,128)}) fusion(f32[2048]{0:T(1024)S(1)} %bitcast.316, bf16[1024,2048]{1,0:T(8,128)(2,1)} %all-gather.19.cloned.1.call-done, bf16[2048,2048]{1,0:T(8,128)(2,1)} %all-gather.21.cloned.1.call-done), kind=kOutput, calls=%fused_computation.67.clone.1 | convolution fusion | flops 8728346624 | bytes 25174016 | tf_op jit(solution)/shard_map/while/body/eval_jaxpr/dot_general | solution.py:174
  626.3 42.8 %reduce-scatter.25.cloned.1.call-done = f32[256,2048]{1,0:T(8,128)} async-done(((f32[1024,2048]{1,0:T(8,128)}), f32[256,2048]{1,0:T(8,128)}) %reduce-scatter.25.cloned.1.call-update) | async-done | bytes 2097168 | tf_op jit(solution)/shard_map/while/body/eval_jaxpr/reduce_scatter | solution.py:266
  669.1 147.6 %reduce-scatter.23.cloned.1.call-done = f32[256,2048]{1,0:T(8,128)} async-done(((f32[1024,2048]{1,0:T(8,128)}), f32[256,2048]{1,0:T(8,128)}) %reduce-scatter.23.cloned.1.call-update) | async-done | bytes 2097168 | tf_op jit(solution)/shard_map/while/body/eval_jaxpr/reduce_scatter | solution.py:267
  821.1 143.1 %reduce-scatter.27.cloned.1.call-done = f32[256,2048]{1,0:T(8,128)} async-done(((f32[1024,2048]{1,0:T(8,128)}), f32[256,2048]{1,0:T(8,128)}) %reduce-scatter.27.cloned.1.call-update) | async-done | bytes 2097168 | tf_op jit(solution)/shard_map/while/body/eval_jaxpr/reduce_scatter | solution.py:179
  981.5 25.4 %collective-permute-done = bf16[256,2048]{1,0:T(8,128)(2,1)S(1)} collective-permute-done((bf16[256,2048]{1,0:T(8,128)(2,1)S(1)}, bf16[256,2048]{1,0:T(8,128)(2,1)S(1)}, u32[]{:S(2)}, u32[]{:S(2)}) %collective-permute-start) | collective-permute-done | bytes 1048608 | tf_op jit(solution)/shard_map/while/body/eval_jaxpr/ppermute | solution.py:186
  1006.9 45.7 %collective-permute-done.1 = bf16[256,2048]{1,0:T(8,128)(2,1)} collective-permute-done((bf16[256,2048]{1,0:T(8,128)(2,1)S(1)}, bf16[256,2048]{1,0:T(8,128)(2,1)}, u32[]{:S(2)}, u32[]{:S(2)}) %collective-permute-start.1) | collective-permute-done | bytes 1048608 | tf_op jit(solution)/shard_map/while/body/eval_jaxpr/ppermute | solution.py:186
  1083.8 30.9 %collective-permute-done.2 = bf16[256,2048]{1,0:T(8,128)(2,1)} collective-permute-done((bf16[256,2048]{1,0:T(8,128)(2,1)}, bf16[256,2048]{1,0:T(8,128)(2,1)}, u32[]{:S(2)}, u32[]{:S(2)}) %collective-permute-start.2) | collective-permute-done | bytes 1048608 | tf_op jit(solution)/shard_map/while/body/eval_jaxpr/ppermute | solution.py:186
  1134.9 34.6 %all-gather.13.cloned.1.call-done = bf16[2048,2,768]{0,2,1:T(8,128)(2,1)} async-done(((bf16[256,2,768]{0,2,1:T(8,128)(2,1)}), bf16[2048,2,768]{0,2,1:T(8,128)(2,1)}) %all-gather.13.cloned.1.call-update) | async-done | bytes 6291472 | tf_op jit(solution)/shard_map/while/body/eval_jaxpr/all_gather | solution.py:106
  1206.9 87.6 %while.110 = (s32[]{:T(128)}, f32[1024,2,256]{0,2,1:T(8,128)}, f32[1024,2,256]{0,2,1:T(8,128)}, f32[2,512,2,256]{1,0,3,2:T(2,128)}, s32[2]{0:T(128)S(1)}, /*inde...) while((s32[]{:T(128)}, f32[1024,2,256]{0,2,1:T(8,128)}, ...), condition=%wide.region_9.10_spmd.clone.clone, body=%wide.region_7.9_spmd.clone.clone.sunk | while | flops 2704015360 | bytes 111194568 | solution.py:248
  1223.2 19.7 dynamic_update_slice.48
  1265.7 19.7 dynamic_update_slice.48
  1340.4 31.4 %fusion.255 = (bf16[1024,2048]{1,0:T(8,128)(2,1)}, f32[1024,2048]{1,0:T(8,128)}) fusion(f32[2048]{0:T(1024)S(1)} %bitcast.316, bf16[1024,2048]{1,0:T(8,128)(2,1)} %all-gather.19.cloned.1.call-done, bf16[2048,2048]{1,0:T(8,128)(2,1)} %all-gather.21.cloned.1.call-done), kind=kOutput, calls=%fused_computation.67.clone.1 | convolution fusion | flops 8728346624 | bytes 25174016 | tf_op jit(solution)/shard_map/while/body/eval_jaxpr/dot_general | solution.py:174
  1444.0 18.6 select_add_fusion.26
  1479.0 32.6 %reduce-scatter.25.cloned.1.call-done = f32[256,2048]{1,0:T(8,128)} async-done(((f32[1024,2048]{1,0:T(8,128)}), f32[256,2048]{1,0:T(8,128)}) %reduce-scatter.25.cloned.1.call-update) | async-done | bytes 2097168 | tf_op jit(solution)/shard_map/while/body/eval_jaxpr/reduce_scatter | solution.py:266
  1511.6 147.4 %reduce-scatter.23.cloned.1.call-done = f32[256,2048]{1,0:T(8,128)} async-done(((f32[1024,2048]{1,0:T(8,128)}), f32[256,2048]{1,0:T(8,128)}) %reduce-scatter.23.cloned.1.call-update) | async-done | bytes 2097168 | tf_op jit(solution)/shard_map/while/body/eval_jaxpr/reduce_scatter | solution.py:267
  1663.5 143.0 %reduce-scatter.27.cloned.1.call-done = f32[256,2048]{1,0:T(8,128)} async-done(((f32[1024,2048]{1,0:T(8,128)}), f32[256,2048]{1,0:T(8,128)}) %reduce-scatter.27.cloned.1.call-update) | async-done | bytes 2097168 | tf_op jit(solution)/shard_map/while/body/eval_jaxpr/reduce_scatter | solution.py:179
  1824.6 21.9 copy.230
  1878.8 22.5 %all-to-all-done.3 = bf16[2,1,256,2048]{3,0,1,2:T(2,128)(2,1)S(1)} async-done(((bf16[2,1,256,2048]{3,0,1,2:T(2,128)(2,1)}), bf16[2,1,256,2048]{3,0,1,2:T(2,128)(2,1)S(1)}, u32[]{:S(2)}, u32[]{:S(2)}) %all-to-all-start.3) | async-done | bytes 2097184 | tf_op jit(solution)/shard_map/all_to_all | solution.py:313
  1907.2 64.1 %all-reduce.13 = (f32[2048]{0:T(1024)S(1)}, f32[2048]{0:T(1024)S(1)}, f32[2048]{0:T(1024)S(1)}, f32[2048]{0:T(1024)S(1)}, f32[2048]{0:T(1024)S(1)}, /*index=5*/f32[2048]{0:T(1024)S(1)}) all-reduce(f32[2048]{0:T(1024)S(1)} %copy-done.32, f32[2048]{0:T(1024)S(1)} %copy-done.35, ...), channel_id=5, replica_groups=mesh['dp'=8,'tensor'=4] {'dp','tensor'}, use_global_device_ids=true, to_apply=%region_26.28.clone | all-reduce | flops 12288 | bytes 98304
  1994.6 62.7 %all-reduce.17.cloned.1.call-done = bf16[2048,2,768]{2,1,0:T(2,128)(2,1)} async-done(((bf16[2048,2,768]{2,1,0:T(2,128)(2,1)}), bf16[2048,2,768]{2,1,0:T(2,128)(2,1)}) %all-reduce.17.cloned.1.call-update) | async-done | bytes 6291472
  2060.1 72.0 %reduce-scatter.15.cloned.1.call-done = bf16[256,2048]{1,0:T(8,128)(2,1)} async-done(((bf16[2048,2048]{1,0:T(8,128)(2,1)}), bf16[256,2048]{1,0:T(8,128)(2,1)}) %reduce-scatter.15.cloned.1.call-update) | async-done | bytes 1048592 | tf_op jit(solution)/shard_map/reduce_scatter | solution.py:300
  2134.8 72.2 %reduce-scatter.17.cloned.1.call-done = bf16[2048,256]{1,0:T(8,128)(2,1)} async-done(((bf16[2048,2048]{1,0:T(8,128)(2,1)}), bf16[2048,256]{1,0:T(8,128)(2,1)}) %reduce-scatter.17.cloned.1.call-update) | async-done | bytes 1048592 | tf_op jit(solution)/shard_map/reduce_scatter | solution.py:306
  (641 shorter events, 712.3 us)
Async XLA Ops:
  20.3 31.8 %all-to-all-start = ((bf16[2,8,32,2048]{3,2,0,1:T(8,128)(2,1)}), bf16[2,8,32,2048]{3,2,0,1:T(8,128)(2,1)S(1)}, u32[]{:S(2)}, u32[]{:S(2)}) async-start(bf16[2,8,32,2048]{3,2,0,1:T(8,128)(2,1)} %copy.186), calls=%async_computation.3 | async-start | bytes 4194304 | tf_op jit(solution)/shard_map/all_to_all | solution.py:88
  52.1 72.3 %all-to-all-start.1 = ((bf16[2,8,32,2048]{3,2,0,1:T(8,128)(2,1)}), bf16[2,8,32,2048]{3,2,0,1:T(8,128)(2,1)}, u32[]{:S(2)}, u32[]{:S(2)}) async-start(bf16[2,8,32,2048]{3,2,0,1:T(8,128)(2,1)} %copy.188), calls=%async_computation.4 | async-start | bytes 4194304 | tf_op jit(solution)/shard_map/all_to_all | solution.py:89
  127.6 157.2 %all-gather.17.cloned.1.call-start = ((), (), s32[]{:S(2)}) async-start(), calls=%async_computation.20 | async-start | bytes 2359296 | tf_op jit(solution)/shard_map/while/body/eval_jaxpr/all_gather | solution.py:108
  128.3 163.0 %all-gather.15.cloned.1.call-start = ((), (), s32[]{:S(2)}) async-start(), calls=%async_computation.19 | async-start | bytes 5242880 | tf_op jit(solution)/shard_map/while/body/eval_jaxpr/all_gather | solution.py:141
  134.9 192.1 %all-gather.13.cloned.1.call-start = ((), (), s32[]{:S(2)}) async-start(), calls=%async_computation.18 | async-start | bytes 7077888 | tf_op jit(solution)/shard_map/while/body/eval_jaxpr/all_gather | solution.py:106
  135.6 362.3 %all-gather.19.cloned.1.call-start = ((), (), s32[]{:S(2)}) async-start(), calls=%async_computation.21 | async-start | bytes 5242880 | tf_op jit(solution)/shard_map/while/body/eval_jaxpr/all_gather | solution.py:142
  136.2 361.7 %all-gather.21.cloned.1.call-start = ((), (), s32[]{:S(2)}) async-start(), calls=%async_computation.22 | async-start | bytes 9437184 | tf_op jit(solution)/shard_map/while/body/eval_jaxpr/all_gather | solution.py:109
  136.8 392.3 %all-gather.23.cloned.1.call-start = ((), (), s32[]{:S(2)}) async-start(), calls=%async_computation.23 | async-start | bytes 9437184 | tf_op jit(solution)/shard_map/while/body/eval_jaxpr/all_gather | solution.py:111
  164.9 46.1 %collective-permute-start.1 = (bf16[256,2048]{1,0:T(8,128)(2,1)S(1)}, bf16[256,2048]{1,0:T(8,128)(2,1)}, u32[]{:S(2)}, u32[]{:S(2)}) collective-permute-start(bf16[256,2048]{1,0:T(8,128)(2,1)S(1)} %collective-permute-done), channel_id=1, source_target_pairs={{0,1},{1,2},{2,3},{3,0},{4,5},{5,6},{6,7},{7,4},{8,9},{9,10},{10,1... | collective-permute-start | bytes 3145736 | tf_op jit(solution)/shard_map/while/body/eval_jaxpr/ppermute | solution.py:186
  211.0 60.3 %collective-permute-start.2 = (bf16[256,2048]{1,0:T(8,128)(2,1)}, bf16[256,2048]{1,0:T(8,128)(2,1)}, u32[]{:S(2)}, u32[]{:S(2)}) collective-permute-start(bf16[256,2048]{1,0:T(8,128)(2,1)} %collective-permute-done.1), channel_id=1, source_target_pairs={{0,1},{1,2},{2,3},{3,0},{4,5},{5,6},{6,7},{7,4},{8,9},{9,10},{10,1... | collective-permute-start | bytes 3145736 | tf_op jit(solution)/shard_map/while/body/eval_jaxpr/ppermute | solution.py:186
  218.3 450.7 %reduce-scatter.25.cloned.1.call-start = ((), (), s32[]{:S(2)}) async-start(), calls=%async_computation.25 | async-start | bytes 10485760 | tf_op jit(solution)/shard_map/while/body/eval_jaxpr/reduce_scatter | solution.py:266
  488.7 328.0 %reduce-scatter.23.cloned.1.call-start = ((), (), s32[]{:S(2)}) async-start(), calls=%async_computation.24 | async-start | bytes 10485760 | tf_op jit(solution)/shard_map/while/body/eval_jaxpr/reduce_scatter | solution.py:267
  560.8 403.4 %reduce-scatter.27.cloned.1.call-start = ((), (), s32[]{:S(2)}) async-start(), calls=%async_computation.26 | async-start | bytes 10485760 | tf_op jit(solution)/shard_map/while/body/eval_jaxpr/reduce_scatter | solution.py:179
  969.3 158.9 %all-gather.17.cloned.1.call-start = ((), (), s32[]{:S(2)}) async-start(), calls=%async_computation.20 | async-start | bytes 2359296 | tf_op jit(solution)/shard_map/while/body/eval_jaxpr/all_gather | solution.py:108
  969.9 165.1 %all-gather.15.cloned.1.call-start = ((), (), s32[]{:S(2)}) async-start(), calls=%async_computation.19 | async-start | bytes 5242880 | tf_op jit(solution)/shard_map/while/body/eval_jaxpr/all_gather | solution.py:141
  976.4 193.2 %all-gather.13.cloned.1.call-start = ((), (), s32[]{:S(2)}) async-start(), calls=%async_computation.18 | async-start | bytes 7077888 | tf_op jit(solution)/shard_map/while/body/eval_jaxpr/all_gather | solution.py:106
  977.0 363.4 %all-gather.19.cloned.1.call-start = ((), (), s32[]{:S(2)}) async-start(), calls=%async_computation.21 | async-start | bytes 5242880 | tf_op jit(solution)/shard_map/while/body/eval_jaxpr/all_gather | solution.py:142
  977.7 362.6 %all-gather.21.cloned.1.call-start = ((), (), s32[]{:S(2)}) async-start(), calls=%async_computation.22 | async-start | bytes 9437184 | tf_op jit(solution)/shard_map/while/body/eval_jaxpr/all_gather | solution.py:109
  978.3 393.4 %all-gather.23.cloned.1.call-start = ((), (), s32[]{:S(2)}) async-start(), calls=%async_computation.23 | async-start | bytes 9437184 | tf_op jit(solution)/shard_map/while/body/eval_jaxpr/all_gather | solution.py:111
  1006.9 45.8 %collective-permute-start.1 = (bf16[256,2048]{1,0:T(8,128)(2,1)S(1)}, bf16[256,2048]{1,0:T(8,128)(2,1)}, u32[]{:S(2)}, u32[]{:S(2)}) collective-permute-start(bf16[256,2048]{1,0:T(8,128)(2,1)S(1)} %collective-permute-done), channel_id=1, source_target_pairs={{0,1},{1,2},{2,3},{3,0},{4,5},{5,6},{6,7},{7,4},{8,9},{9,10},{10,1... | collective-permute-start | bytes 3145736 | tf_op jit(solution)/shard_map/while/body/eval_jaxpr/ppermute | solution.py:186
  1052.7 62.0 %collective-permute-start.2 = (bf16[256,2048]{1,0:T(8,128)(2,1)}, bf16[256,2048]{1,0:T(8,128)(2,1)}, u32[]{:S(2)}, u32[]{:S(2)}) collective-permute-start(bf16[256,2048]{1,0:T(8,128)(2,1)} %collective-permute-done.1), channel_id=1, source_target_pairs={{0,1},{1,2},{2,3},{3,0},{4,5},{5,6},{6,7},{7,4},{8,9},{9,10},{10,1... | collective-permute-start | bytes 3145736 | tf_op jit(solution)/shard_map/while/body/eval_jaxpr/ppermute | solution.py:186
  1071.2 440.4 %reduce-scatter.25.cloned.1.call-start = ((), (), s32[]{:S(2)}) async-start(), calls=%async_computation.25 | async-start | bytes 10485760 | tf_op jit(solution)/shard_map/while/body/eval_jaxpr/reduce_scatter | solution.py:266
  1330.9 328.1 %reduce-scatter.23.cloned.1.call-start = ((), (), s32[]{:S(2)}) async-start(), calls=%async_computation.24 | async-start | bytes 10485760 | tf_op jit(solution)/shard_map/while/body/eval_jaxpr/reduce_scatter | solution.py:267
  1403.2 403.3 %reduce-scatter.27.cloned.1.call-start = ((), (), s32[]{:S(2)}) async-start(), calls=%async_computation.26 | async-start | bytes 10485760 | tf_op jit(solution)/shard_map/while/body/eval_jaxpr/reduce_scatter | solution.py:179
  1817.3 157.5 %reduce-scatter.19.cloned.1.call-start = ((), (), s32[]{:S(2)}) async-start(), calls=%async_computation.15 | async-start | bytes 221184
  1818.9 157.2 %reduce-scatter.21.cloned.1.call-start = ((), (), s32[]{:S(2)}) async-start(), calls=%async_computation.16 | async-start | bytes 294912
  1820.6 172.0 %reduce-scatter.13.cloned.1.call-start = ((), (), s32[]{:S(2)}) async-start(), calls=%async_computation.12 | async-start | bytes 2359296 | tf_op jit(solution)/shard_map/reduce_scatter | solution.py:297
  1824.5 232.8 %all-reduce.17.cloned.1.call-start = ((), (), s32[]{:S(2)}) async-start(), calls=%async_computation.17 | async-start | bytes 12582912
  1846.5 285.6 %reduce-scatter.15.cloned.1.call-start = ((), (), s32[]{:S(2)}) async-start(), calls=%async_computation.13 | async-start | bytes 9437184 | tf_op jit(solution)/shard_map/reduce_scatter | solution.py:300
  1855.7 351.4 %reduce-scatter.17.cloned.1.call-start = ((), (), s32[]{:S(2)}) async-start(), calls=%async_computation.14 | async-start | bytes 9437184 | tf_op jit(solution)/shard_map/reduce_scatter | solution.py:306
  1869.9 31.4 %all-to-all-start.3 = ((bf16[2,1,256,2048]{3,0,1,2:T(2,128)(2,1)}), bf16[2,1,256,2048]{3,0,1,2:T(2,128)(2,1)S(1)}, u32[]{:S(2)}, u32[]{:S(2)}) async-start(bf16[2,1,256,2048]{3,0,1,2:T(2,128)(2,1)} %bitcast.307), calls=%async_computation.6 | async-start | bytes 4194304 | tf_op jit(solution)/shard_map/all_to_all | solution.py:313
  1901.3 82.1 %all-to-all-start.2 = ((bf16[2,1,256,2048]{3,0,1,2:T(2,128)(2,1)}), bf16[2,1,256,2048]{3,0,1,2:T(2,128)(2,1)}, u32[]{:S(2)}, u32[]{:S(2)}) async-start(bf16[2,1,256,2048]{3,0,1,2:T(2,128)(2,1)} %bitcast.306), calls=%async_computation.5 | async-start | bytes 4194304 | tf_op jit(solution)/shard_map/all_to_all | solution.py:312
  (134 other events, 8234.6 us)
Sparse Core Ops, SparseCore 0:
  130.3 26.9 all-gather.16
  158.9 121.2 all-gather.14
  282.1 44.8 all-gather.12
  329.0 80.7 all-gather.18
  411.5 52.9 all-gather.20
  466.2 55.9 all-gather.22
  524.6 144.4 reduce-scatter.24
  671.4 145.1 reduce-scatter.22
  819.0 145.1 reduce-scatter.26
  971.7 28.6 all-gather.16
  1001.9 120.8 all-gather.14
  1124.6 44.9 all-gather.12
  1171.7 80.7 all-gather.18
  1254.2 52.9 all-gather.20
  1308.9 55.9 all-gather.22
  1367.1 144.4 reduce-scatter.24
  1513.8 145.1 reduce-scatter.22
  1661.3 145.1 reduce-scatter.26
Sparse Core Ops, SparseCore 1:
  1821.4 34.2 reduce-scatter.18
  1859.4 34.6 reduce-scatter.20
  1897.3 52.0 reduce-scatter.12
  1952.9 104.3 all-reduce.16
  2060.8 71.2 reduce-scatter.14
  2135.9 71.1 reduce-scatter.16
